TPU v7x, 32 devices: a whole 2x2x4 slice. The times are simulated.
32 devices in a mesh: chan: 16 (over z, y, x), day: 2 (over core).
Axes of the slice: x: 2, y: 2, z: 4, core: 2. Of those that a mesh axis runs over, the one named last changes fastest.
Arguments:
- spectra: bfloat16 [512, 64, 400], P('chan', 'day'), may hold values from -6 to 6
- owners: int32 [2], replicated, may hold values from 0 to 15
Outputs:
- stacks: bfloat16 [2, 512, 32, 400], P(None, ('chan', 'day'))
Inputs may be any that keep to these rules, and one draw needn't show every extreme that they name: `owners`: block indices along the channel axis; two steps may name the same block.
All inputs are finite; a program needn't handle non-finite values.
Results may differ from a plain program's by a relative error of at most 0.0073.
Values may be sent and summed in bfloat16 or wider, within the bound.
A program may use at most 64 MiB of HBM per device.

v0:
```python
import math

import jax
import jax.numpy as jnp
from jax import lax
from jax.sharding import PartitionSpec as P

LAGS = 400
STEPS = 2


def broadcast(array, axis, root):
    mine = lax.axis_index(axis) == root
    return lax.psum(jnp.where(mine, array, jnp.zeros_like(array)), axis)


def whiten(spectra, bins):
    values = spectra.astype(jnp.float32)
    real_part = values[..., :bins]
    imag_part = values[..., bins:]
    power = real_part * real_part + imag_part * imag_part
    mean_power = jnp.mean(power, axis=-1, keepdims=True)
    factor = lax.rsqrt(power + 0.25 * mean_power + 1e-06)
    return jnp.concatenate([real_part * factor, imag_part * factor], axis=-1).astype(jnp.bfloat16)


def lag_table(bins, lag_count):
    freqs = jnp.arange(bins, dtype=jnp.int32)
    shifts = jnp.arange(lag_count, dtype=jnp.int32) - lag_count // 2
    phase = jnp.mod(freqs[:, None] * shifts[None, :], 2 * bins)
    angle = phase.astype(jnp.float32) * (math.pi / bins)
    return jnp.concatenate([jnp.cos(angle), -jnp.sin(angle)], axis=0).astype(jnp.bfloat16)


def day_cross(own, other, bins):
    own_re, own_im = (own[..., :bins], own[..., bins:])
    oth_re, oth_im = (other[..., :bins], other[..., bins:])
    cross_re = jnp.einsum("iwf,jwf->ijf", own_re, oth_re, preferred_element_type=jnp.float32)
    cross_re = cross_re + jnp.einsum(
        "iwf,jwf->ijf", own_im, oth_im, preferred_element_type=jnp.float32
    )
    cross_im = jnp.einsum("iwf,jwf->ijf", own_im, oth_re, preferred_element_type=jnp.float32)
    cross_im = cross_im - jnp.einsum(
        "iwf,jwf->ijf", own_re, oth_im, preferred_element_type=jnp.float32
    )
    cross = jnp.concatenate([cross_re, cross_im], axis=-1).astype(jnp.bfloat16)
    return cross.astype(jnp.float32)


def apply_lags(summed, table, norm):
    kept = summed.astype(jnp.bfloat16)
    rows = kept.shape[0] * kept.shape[1]
    lagged = (
        jnp.dot(kept.reshape(rows, kept.shape[2]), table, preferred_element_type=jnp.float32) * norm
    )
    return lagged.reshape(kept.shape[0], kept.shape[1], table.shape[1]).astype(jnp.bfloat16)


def local(spectra, owners):
    bins = spectra.shape[-1] // 2
    windows_all = spectra.shape[1] * lax.axis_size("day")
    white = whiten(spectra, bins)
    table = lag_table(bins, LAGS)
    norm = 1.0 / math.sqrt(windows_all * bins)
    result_steps = []
    for step in range(STEPS):
        block = broadcast(white, "chan", owners[step])
        crossed = day_cross(white, block, bins)
        summed = lax.psum_scatter(
            crossed.astype(jnp.bfloat16), "day", scatter_dimension=0, tiled=True
        ).astype(jnp.float32)
        result_steps.append(apply_lags(summed, table, norm))
    return jnp.stack(result_steps, axis=0)


def solution(mesh):
    placed = (P("chan", "day", None), P())
    return jax.shard_map(
        local,
        mesh=mesh,
        in_specs=placed,
        out_specs=P(None, ("chan", "day"), None, None),
        check_vma=False,
    )
```

profile of v0, /device:TPU:0, one launch (start us, length us, event | category | flops | bytes accessed | tf_op | source)
XLA Modules:
  0.0 300.6 jit_solution(8346272925173790976)
XLA Ops:
  6.5 0.0 all-reduce.3.cloned.1.call-start
  6.5 1.5 convert_element_type.46
  8.0 0.5 fusion.13
  8.6 0.6 multiply_convert_fusion.1
  9.2 0.0 copy-start.11
  9.2 0.0 copy-start.12
  9.2 0.0 copy-start.14
  9.2 0.8 copy-done.11
  10.0 0.2 copy-done.12
  10.2 1.4 pad_maximum_fusion
  11.6 3.7 %copy.11 = bf16[32,32,400]{1,0,2:T(8,128)(2,1)S(1)} copy(bf16[32,32,400]{2,1,0:T(8,128)(2,1)} %pad_maximum_fusion) | data formatting | bytes 1638400 | tf_op jit(solution)/shard_map/concatenate | solution.py:24
  15.2 0.0 copy-done.14
  15.3 0.7 fusion.14
  17.3 3.2 %broadcast_select_fusion.1 = (bf16[32,32,400]{1,0,2:T(8,128)(2,1)}, bf16[32,32,400]{1,0,2:T(8,128)(2,1)}) fusion(bf16[32,32,400]{1,0,2:T(8,128)(2,1)S(1)} %copy.11, pred[]{:T(512)S(6)} %eq.8, pred[]{:T(512)S(6)} %eq.9), kind=kLoop, calls=%fused_computation.5 | loop fusion | flops 819200 | bytes 2457602 | tf_op jit(solution)/shard_map/jit(_where)/select_n | solution.py:14
  20.4 0.0 copy-start.13
  20.4 0.0 all-reduce.3.cloned.1.call-update
  20.4 0.0 reduce-scatter.3.cloned.1.call-start
  20.5 1.0 copy-done.13
  21.5 1.5 copy.12
  22.9 0.0 copy-start.4
  23.0 2.6 copy.13
  25.5 0.0 copy-start.6
  25.5 213.4 %all-reduce.3.cloned.1.call-done = (bf16[32,32,400]{1,0,2:T(8,128)(2,1)}, bf16[32,32,400]{1,0,2:T(8,128)(2,1)}) async-done(((bf16[32,32,400]{1,0,2:T(8,128)(2,1)}, bf16[32,32,400]{1,0,2:T(8,128)(2,1)}), (bf16[32,32,400]{1,0,2:T(8,128)(2,1)}, bf16[32,32,400]{1,0,2:T(8,128)(2,1)})) %all-reduce.3.cloned.1.call-update) | async-done | bytes 1638416 | tf_op jit(solution)/shard_map/psum | solution.py:14
  238.9 0.0 copy-start.2
  238.9 4.2 %fusion.15 = f32[200,32,32]{2,1,0:T(8,128)} fusion(bf16[32,32,400]{1,0,2:T(8,128)(2,1)} %get-tuple-element.6, bf16[32,32,200]{1,0,2:T(8,128)(2,1)S(1)} %copy.12), kind=kOutput, calls=%fused_computation.38 | convolution fusion | flops 13107200 | bytes 2048000 | tf_op jit(solution)/shard_map/iwf,jwf->ijf/dot_general | solution.py:38
  243.2 0.0 copy-done.6
  243.2 0.0 copy-done.2
  243.2 0.0 copy-start
  243.2 2.7 fusion.16
  245.8 0.0 copy-done.4
  245.8 0.0 copy-done
  245.8 0.0 copy-start.7
  245.8 2.7 fusion.17
  248.5 0.0 copy-done.7
  248.6 2.7 fusion.18
  251.3 0.0 copy-done.3
  251.3 1.4 copy-done.9
  252.7 2.1 fusion
  254.8 3.8 %copy.16 = bf16[32,32,200]{2,1,0:T(8,128)(2,1)} copy(bf16[32,32,200]{0,1,2:T(8,128)(2,1)} %fusion) | data formatting | bytes 819200 | tf_op jit(solution)/shard_map/add | solution.py:39
  258.6 4.6 %fusion.1 = bf16[32,32,200]{0,1,2:T(8,128)(2,1)} fusion(f32[200,32,32]{2,1,0:T(8,128)} %fusion.16, bf16[32,32,400]{1,0,2:T(8,128)(2,1)S(1)} %copy-done.3, bf16[32,32,200]{1,0,2:T(8,128)(2,1)} %copy-done.4), kind=kOutput, calls=%fused_computation.7 | convolution fusion | flops 13516800 | bytes 2457600 | tf_op jit(solution)/shard_map/iwf,jwf->ijf/dot_general | solution.py:43
  263.2 4.0 %copy.17 = bf16[32,32,200]{2,1,0:T(8,128)(2,1)} copy(bf16[32,32,200]{0,1,2:T(8,128)(2,1)} %fusion.1) | data formatting | bytes 819200 | tf_op jit(solution)/shard_map/sub | solution.py:43
  267.2 2.6 pad_maximum_fusion.1
  269.8 0.0 reduce-scatter.3.cloned.1.call-update
  269.8 0.2 reduce-scatter.5.cloned.1.call-start
  270.0 0.0 copy-done.1
  270.0 0.0 copy-start.5
  270.1 0.0 copy-start.8
  270.1 4.7 %fusion.2 = bf16[32,32,200]{0,1,2:T(8,128)(2,1)} fusion(f32[200,32,32]{2,1,0:T(8,128)} %fusion.17, bf16[32,32,400]{1,0,2:T(8,128)(2,1)S(1)} %copy-done.1, bf16[32,32,200]{1,0,2:T(8,128)(2,1)} %copy-done.6), kind=kOutput, calls=%fused_computation.8 | convolution fusion | flops 13516800 | bytes 2457600 | tf_op jit(solution)/shard_map/iwf,jwf->ijf/dot_general | solution.py:39
  274.8 0.0 copy-done.5
  274.8 0.0 copy-done.8
  274.8 2.1 fusion.3
  276.9 3.3 %copy.24 = bf16[32,32,200]{2,1,0:T(8,128)(2,1)S(1)} copy(bf16[32,32,200]{0,1,2:T(8,128)(2,1)} %fusion.2) | data formatting | bytes 819200 | tf_op jit(solution)/shard_map/add | solution.py:39
  280.2 0.0 copy-done.10
  280.3 1.9 copy.25
  282.1 1.4 pad_maximum_fusion.2
  283.5 0.0 reduce-scatter.5.cloned.1.call-update
  283.6 1.8 cosine_convert_fusion
  285.3 0.0 reduce-scatter.3.cloned.1.call-done
  285.4 1.5 fusion.4
  286.8 0.2 copy.18
  287.1 4.2 %reduce-scatter.5.cloned.1.call-done = bf16[16,32,400]{2,1,0:T(8,128)(2,1)} async-done(((bf16[32,32,400]{2,1,0:T(8,128)(2,1)}), bf16[16,32,400]{2,1,0:T(8,128)(2,1)}) %reduce-scatter.5.cloned.1.call-update) | async-done | bytes 409616 | tf_op jit(solution)/shard_map/reduce_scatter | solution.py:69
  291.2 1.5 fusion.5
  292.7 0.2 copy.26
  292.9 1.1 pad_maximum_fusion.3
  (6 shorter events, 0.0 us)
Async XLA Ops:
  6.5 232.4 %all-reduce.3.cloned.1.call-start = ((), (), s32[]{:S(2)}) async-start(), calls=%async_computation.4 | async-start | bytes 13107200 | tf_op jit(solution)/shard_map/psum | solution.py:14
  9.2 0.8 copy-start.11
  9.2 1.0 copy-start.12
  9.2 6.0 %copy-start.14 = (s32[2]{0:T(128)S(1)}, s32[2]{0:T(128)}, u32[]{:S(2)}) copy-start(s32[2]{0:T(128)} %param.3) | copy-start | bytes 28
  20.4 1.0 copy-start.13
  20.4 264.9 %reduce-scatter.3.cloned.1.call-start = ((), (), s32[]{:S(2)}) async-start(), calls=%async_computation.2 | async-start | bytes 1572864 | tf_op jit(solution)/shard_map/reduce_scatter | solution.py:69
  22.9 222.9 %copy-start.4 = (bf16[32,32,200]{1,0,2:T(8,128)(2,1)}, bf16[32,32,200]{1,0,2:T(8,128)(2,1)S(1)}, u32[]{:S(2)}) copy-start(bf16[32,32,200]{1,0,2:T(8,128)(2,1)S(1)} %copy.12) | copy-start | bytes 1228804
  25.5 217.6 %copy-start.6 = (bf16[32,32,200]{1,0,2:T(8,128)(2,1)}, bf16[32,32,200]{1,0,2:T(8,128)(2,1)S(1)}, u32[]{:S(2)}) copy-start(bf16[32,32,200]{1,0,2:T(8,128)(2,1)S(1)} %copy.13) | copy-start | bytes 1228804
  238.9 4.2 %copy-start.2 = (bf16[32,32,400]{1,0,2:T(8,128)(2,1)S(1)}, bf16[32,32,400]{1,0,2:T(8,128)(2,1)}, u32[]{:S(2)}) copy-start(bf16[32,32,400]{1,0,2:T(8,128)(2,1)} %get-tuple-element.6) | copy-start | bytes 2457604
  243.2 2.7 copy-start
  245.8 2.7 copy-start.7
  248.5 2.7 copy-start.3
  248.5 4.1 %copy-start.9 = (f32[200,32,32]{2,1,0:T(8,128)S(1)}, f32[200,32,32]{2,1,0:T(8,128)}, u32[]{:S(2)}) copy-start(f32[200,32,32]{2,1,0:T(8,128)} %fusion.15) | copy-start | bytes 2457604
  263.2 6.9 %copy-start.1 = (bf16[32,32,400]{1,0,2:T(8,128)(2,1)S(1)}, bf16[32,32,400]{1,0,2:T(8,128)(2,1)}, u32[]{:S(2)}) copy-start(bf16[32,32,400]{1,0,2:T(8,128)(2,1)} %get-tuple-element.5) | copy-start | bytes 2457604
  269.8 21.4 %reduce-scatter.5.cloned.1.call-start = ((), (), s32[]{:S(2)}) async-start(), calls=%async_computation.3 | async-start | bytes 1572864 | tf_op jit(solution)/shard_map/reduce_scatter | solution.py:69
  270.0 4.7 %copy-start.5 = (bf16[32,32,200]{1,0,2:T(8,128)(2,1)S(1)}, bf16[32,32,200]{1,0,2:T(8,128)(2,1)}, u32[]{:S(2)}) copy-start(bf16[32,32,200]{1,0,2:T(8,128)(2,1)} %copy-done.4) | copy-start | bytes 1228804
  270.1 4.7 %copy-start.8 = (f32[200,32,32]{2,1,0:T(8,128)S(1)}, f32[200,32,32]{2,1,0:T(8,128)}, u32[]{:S(2)}) copy-start(f32[200,32,32]{2,1,0:T(8,128)} %fusion.18) | copy-start | bytes 2457604
  276.9 3.3 %copy-start.10 = (bf16[32,32,200]{0,1,2:T(8,128)(2,1)S(1)}, bf16[32,32,200]{0,1,2:T(8,128)(2,1)}, u32[]{:S(2)}) copy-start(bf16[32,32,200]{0,1,2:T(8,128)(2,1)} %fusion.3) | copy-start | bytes 1228804
Sparse Core Ops, SparseCore 0:
  20.6 218.3 all-reduce.2
  269.9 7.4 reduce-scatter.2
  283.7 7.5 reduce-scatter.4
where the time goes:
time: 301 us
  waiting for transfers between devices  218 us (72%)
  matrix products  28.8 us (10%)
  local copies, waits for them, and re-layouts  25.2 us (8%)
  between operations  14.7 us (5%)
  other arithmetic  14 us (5%)
    psum x1, waiting for transfers between devices, broadcast(): return lax.psum(jnp.where(mine, array, jnp.zeros_like(array)), axis)  213 us
    add x2, local copies, waits for them, and re-layouts, day_cross(): cross_re + jnp.einsum('iwf,jwf->ijf', own_im, oth_im, preferred_element_t...  7.15 us
    dot_general x2, matrix products, day_cross(): jnp.einsum('iwf,jwf->ijf', own_re, oth_re, preferred_element_type=jnp.flo...  6.94 us
    dot_general x2, matrix products, day_cross(): jnp.einsum('iwf,jwf->ijf', own_im, oth_im, preferred_element_type=jnp.flo...  6.86 us
    dot_general x2, matrix products, day_cross(): jnp.einsum('iwf,jwf->ijf', own_re, oth_im, preferred_element_type=jnp.flo...  6.69 us
  transfers between devices with their start and end apart: 3, of which 2 were waited for; matrix products, arithmetic and copies ran while one was open for 7% of the time, Pallas kernels for 0%

commit v1 on v0

v1 whole, which is shorter than its diff:
```python
import functools
import math

import jax
import jax.numpy as jnp
import numpy as np
from jax import lax
from jax.experimental import pallas as pl
from jax.experimental.pallas import tpu as pltpu
from jax.sharding import PartitionSpec as P

LAGS = 400
STEPS = 2
MESH_ID = pl.DeviceIdType.MESH


def whiten(spectra, bins):
    values = spectra.astype(jnp.float32)
    real_part = values[..., :bins]
    imag_part = values[..., bins:]
    power = real_part * real_part + imag_part * imag_part
    mean_power = jnp.mean(power, axis=-1, keepdims=True)
    factor = lax.rsqrt(power + 0.25 * mean_power + 1e-06)
    return (
        (real_part * factor).astype(jnp.bfloat16),
        (imag_part * factor).astype(jnp.bfloat16),
    )


def lag_table(bins, lag_count):
    freqs = np.arange(bins, dtype=np.int64)
    shifts = np.arange(lag_count, dtype=np.int64) - lag_count // 2
    phase = np.mod(freqs[:, None] * shifts[None, :], 2 * bins)
    angle = phase.astype(np.float32) * np.float32(math.pi / bins)
    return np.concatenate([np.cos(angle), -np.sin(angle)], axis=0).astype(jnp.bfloat16)


def chunks_of(piece):
    for count in (5, 4, 2):
        if piece % (count * 16) == 0:
            return count
    return 1


def kernel(
    line, chunks, chans, groups,
    owners_ref, a_ref, b_ref, o_ref,
    w_ref, r1_ref, s2_ref, r2_ref, zout_ref, zin_ref, c_send, c_recv,
    send_sem, recv_sem, day_send, day_recv,
):
    me = lax.axis_index("chan")
    day = lax.axis_index("day")
    cx = lax.rem(me, 2)
    cy = lax.rem(me // 2, 2)
    cz = me // 4
    nx = me + 1 - 2 * cx
    ny = me + 2 - 4 * cy
    rows = a_ref.shape[0]
    piece = rows // 4
    size = piece // chunks

    has_left = cz > 0
    has_right = cz < line - 1

    barrier = pltpu.get_barrier_semaphore()
    pl.semaphore_signal(barrier, inc=1, device_id={"chan": nx}, device_id_type=MESH_ID)
    pl.semaphore_signal(barrier, inc=1, device_id={"chan": ny}, device_id_type=MESH_ID)
    pl.semaphore_signal(barrier, inc=1, device_id={"day": 1 - day}, device_id_type=MESH_ID)

    @pl.when(has_left)
    def _():
        pl.semaphore_signal(barrier, inc=1, device_id={"chan": me - 4}, device_id_type=MESH_ID)

    @pl.when(has_right)
    def _():
        pl.semaphore_signal(barrier, inc=1, device_id={"chan": me + 4}, device_id_type=MESH_ID)

    inside = jnp.logical_and(has_left, has_right)

    @pl.when(inside)
    def _():
        pl.semaphore_wait(barrier, 5)

    @pl.when(jnp.logical_not(inside))
    def _():
        pl.semaphore_wait(barrier, 4 if line > 1 else 3)

    coords = ((cx, cy, nx, ny), (cy, cx, ny, nx))
    hits = []
    for step in range(STEPS):
        owner = owners_ref[step]
        ox = lax.rem(owner, 2)
        oy = lax.rem(owner // 2, 2)
        oz = owner // 4
        first = ox == cx if step == 0 else oy == cy
        second = oy == cy if step == 0 else ox == cx
        hits.append((first, second, oz == cz, oz < cz))

    def at(start, k):
        return pl.ds(pl.multiple_of(start + k * size, 16), size)

    def remote(src, dst, step, phase, k, chan):
        return pltpu.make_async_remote_copy(
            src_ref=src, dst_ref=dst,
            send_sem=send_sem.at[step, phase, k], recv_sem=recv_sem.at[step, phase, k],
            device_id={"chan": chan}, device_id_type=MESH_ID,
        )

    def scatter_first(step, part, k):
        ca, cb, na, nb = coords[step]
        pb = 1 - cb if part == 0 else cb
        return remote(
            a_ref.at[at((1 - ca) * 2 * piece + pb * piece, k)],
            r1_ref.at[step, part, pl.ds(k * size, size)], step, part, k, na,
        )

    def scatter_second(step, k):
        nb = coords[step][3]
        here = pl.ds(k * size, size)
        return remote(s2_ref.at[step, here], r2_ref.at[step, here], step, 2, k, nb)

    def along(step, k, up):
        here = pl.ds(k * size, size)
        side = 0 if up else 1
        return remote(
            zout_ref.at[side, step, here], zin_ref.at[side, step, here],
            step, 3 + side, k, me + 4 if up else me - 4,
        )

    def gather(step, k, phase):
        ca, cb, na, nb = coords[step]
        pb = 1 - cb if phase == 7 else cb
        where = at((ca * 2 + pb) * piece, k)
        return remote(
            w_ref.at[step, where], w_ref.at[step, where], step, phase, k, nb if phase == 5 else na
        )

    pairs = [(k, step) for k in range(chunks) for step in range(STEPS)]
    for part in range(2):
        for k, step in pairs:
            scatter_first(step, part, k).start()

    for k, step in pairs:
        ca, cb, _, _ = coords[step]
        scatter_first(step, 0, k).wait_recv()
        s2_ref[step, pl.ds(k * size, size)] = jnp.where(
            hits[step][0],
            a_ref[at(ca * 2 * piece + (1 - cb) * piece, k)],
            r1_ref[step, 0, pl.ds(k * size, size)],
        )
        scatter_second(step, k).start()

    for k, step in pairs:
        ca, cb, _, _ = coords[step]
        here = pl.ds(k * size, size)
        first, second, level, below = hits[step]
        scatter_first(step, 1, k).wait_recv()
        scatter_second(step, k).wait_recv()
        mine = jnp.where(
            second,
            jnp.where(first, a_ref[at((ca * 2 + cb) * piece, k)], r1_ref[step, 1, here]),
            r2_ref[step, here],
        )
        zout_ref[0, step, here] = mine
        zout_ref[1, step, here] = mine
        own = at((ca * 2 + cb) * piece, k)
        w_ref[step, own] = mine

        def upward():
            @pl.when(has_left)
            def _():
                along(step, k, True).wait_recv()
                got = zin_ref[0, step, here]
                zout_ref[0, step, here] = jnp.where(level, zout_ref[0, step, here], got)
                w_ref[step, own] = jnp.where(below, got, w_ref[step, own])

            @pl.when(has_right)
            def _():
                along(step, k, True).start()

        def downward():
            @pl.when(has_right)
            def _():
                along(step, k, False).wait_recv()
                got = zin_ref[1, step, here]
                zout_ref[1, step, here] = jnp.where(level, zout_ref[1, step, here], got)
                w_ref[step, own] = jnp.where(
                    level, w_ref[step, own], jnp.where(below, w_ref[step, own], got)
                )

            @pl.when(has_left)
            def _():
                along(step, k, False).start()

        @pl.when(cz < line // 2)
        def _():
            upward()
            downward()

        @pl.when(cz >= line // 2)
        def _():
            downward()
            upward()

        gather(step, k, 5).start()
        gather(step, k, 6).start()

    for k, step in pairs:
        gather(step, k, 5).wait_recv()
        gather(step, k, 7).start()

    for k, step in pairs:
        gather(step, k, 6).wait_recv()
        gather(step, k, 7).wait_recv()

    half = chans // 2
    keep = day * half
    give = (1 - day) * half
    lanes = lax.broadcasted_iota(jnp.int32, (chans, a_ref.shape[1]), 1)
    low = jnp.where(lanes < a_ref.shape[1] // 2, 1.0, 0.0).astype(jnp.bfloat16)
    high = jnp.where(lanes < a_ref.shape[1] // 2, 0.0, 1.0).astype(jnp.bfloat16)

    def cross(g, carry):
        base = pl.multiple_of(g * chans, 16)
        kept = pl.ds(pl.multiple_of(base + keep, 16), half)
        given = pl.ds(pl.multiple_of(base + give, 16), half)
        left = jnp.concatenate([a_ref[kept], b_ref[kept], a_ref[given], b_ref[given]], axis=0)
        blocks = []
        for step in range(STEPS):
            block = w_ref[step, pl.ds(base, chans)]
            blocks += [block * low, block * high]
        right = jnp.concatenate(blocks, axis=0)
        out = lax.dot_general(
            left, right, (((1,), (1,)), ((), ())), preferred_element_type=jnp.float32
        )
        spot = pl.ds(pl.multiple_of(g * chans, 16), chans)
        o_ref[spot] = out[:chans].astype(jnp.bfloat16)
        c_send[spot] = out[chans:].astype(jnp.bfloat16)
        return carry

    parts = day_send.shape[0]
    per = groups // parts

    def swap(part):
        where = pl.ds(part * per * chans, per * chans)
        return pltpu.make_async_remote_copy(
            src_ref=c_send.at[where], dst_ref=c_recv.at[where],
            send_sem=day_send.at[part], recv_sem=day_recv.at[part],
            device_id={"day": 1 - day}, device_id_type=MESH_ID,
        )

    for part in range(parts):
        lax.fori_loop(part * per, (part + 1) * per, cross, 0, unroll=5)
        swap(part).start()

    for part in range(parts):
        where = pl.ds(part * per * chans, per * chans)
        swap(part).wait_recv()
        total = o_ref[where].astype(jnp.float32) + c_recv[where].astype(jnp.float32)
        o_ref[where] = total.astype(jnp.bfloat16)

    for part in range(parts):
        swap(part).wait_send()
    for k, step in pairs:
        for part in range(2):
            scatter_first(step, part, k).wait_send()
        scatter_second(step, k).wait_send()
        for phase in (5, 6, 7):
            gather(step, k, phase).wait_send()

    @pl.when(has_right)
    def _():
        for k, step in pairs:
            along(step, k, True).wait_send()

    @pl.when(has_left)
    def _():
        for k, step in pairs:
            along(step, k, False).wait_send()


def local(spectra, owners):
    chans, windows, width = spectra.shape
    bins = width // 2
    groups = bins // 2
    line = lax.axis_size("chan") // 4
    windows_all = windows * lax.axis_size("day")
    re_part, im_part = whiten(spectra, bins)

    def packed(first, second):
        both = jnp.stack([first, second], axis=0).reshape(2, chans, windows, 2, groups)
        return both.transpose(4, 1, 3, 0, 2).reshape(groups * chans, 4 * windows)

    plain = packed(re_part, im_part)
    turned = packed(im_part, -re_part)
    rows, lanes = plain.shape
    piece = rows // 4
    chunks = chunks_of(piece)
    bf16 = jnp.bfloat16
    vmem = pl.BlockSpec(memory_space=pltpu.VMEM)
    summed = pl.pallas_call(
        functools.partial(kernel, line, chunks, chans, groups),
        out_shape=jax.ShapeDtypeStruct((groups * chans, 4 * chans), bf16),
        in_specs=[pl.BlockSpec(memory_space=pltpu.SMEM), vmem, vmem],
        out_specs=vmem,
        scratch_shapes=[
            pltpu.VMEM((STEPS, rows, lanes), bf16),
            pltpu.VMEM((STEPS, 2, piece, lanes), bf16),
            pltpu.VMEM((STEPS, piece, lanes), bf16),
            pltpu.VMEM((STEPS, piece, lanes), bf16),
            pltpu.VMEM((2, STEPS, piece, lanes), bf16),
            pltpu.VMEM((2, STEPS, piece, lanes), bf16),
            pltpu.VMEM((groups * chans, 4 * chans), bf16),
            pltpu.VMEM((groups * chans, 4 * chans), bf16),
            pltpu.SemaphoreType.DMA((STEPS, 8, chunks)),
            pltpu.SemaphoreType.DMA((STEPS, 8, chunks)),
            pltpu.SemaphoreType.DMA((4,)),
            pltpu.SemaphoreType.DMA((4,)),
        ],
        compiler_params=pltpu.CompilerParams(collective_id=0, has_side_effects=True),
    )(owners, plain, turned)

    norm = 1.0 / math.sqrt(windows_all * bins)
    table = jnp.asarray(lag_table(bins, LAGS)).reshape(2, 2, groups, LAGS)
    summed = summed.reshape(groups, 2, chans // 2, STEPS, 2, chans)
    lagged = jnp.einsum(
        "gcishj,chgl->sijl", summed, table, preferred_element_type=jnp.float32
    ) * norm
    return lagged.astype(bf16)


def solution(mesh):
    placed = (P("chan", "day", None), P())
    return jax.shard_map(
        local,
        mesh=mesh,
        in_specs=placed,
        out_specs=P(None, ("chan", "day"), None, None),
        check_vma=False,
    )
```

time: 301 us -> 166 us (0.55)
  waiting for transfers between devices: 218 us -> 0 us
  Pallas kernels: 0 us -> 123 us
  matrix products: 28.8 us -> 6.45 us
  between operations: 14.7 us -> 0.12 us
  other arithmetic: 14 us -> 4.96 us
  local copies, waits for them, and re-layouts: 25.2 us -> 30.7 us
    psum x1 -> x0, waiting for transfers between devices: 213 us -> none  [broadcast(): return lax.psum(jnp.where(mine, array, jnp.zeros_like(array)), axis)]
    pallas_call x0 -> x1, Pallas kernels: none -> 123 us  [local(): pl.pallas_call(functools.partial(kernel, line, chunks, chans, groups), ou...]
    reshape x0 -> x5, local copies, waits for them, and re-layouts: none -> 28.4 us  [the longest x4 21.3 us: packed(): return both.transpose(4, 1, 3, 0, 2).reshape(groups * chans, 4 * windows)]
    dot_general x10 -> x1, matrix products: 28.8 us -> 6.45 us  [local(): jnp.einsum('gcishj,chgl->sijl', summed, table, preferred_element_type=jnp...]
    add x2 -> x0, local copies, waits for them, and re-layouts: 7.15 us -> none  [day_cross(): cross_re + jnp.einsum('iwf,jwf->ijf', own_im, oth_im, preferred_element_t...]
    sub x2 -> x0, local copies, waits for them, and re-layouts: 5.87 us -> none  [day_cross(): cross_im - jnp.einsum('iwf,jwf->ijf', own_re, oth_im, preferred_element_t...]
    concatenate x3 -> x0, other arithmetic: 5.39 us -> none  [the longest x2 3.99 us: day_cross(): cross = jnp.concatenate([cross_re, cross_im], axis=-1).astype(jnp.bfloat16)]
    slice x3 -> x0, local copies, waits for them, and re-layouts: 4.72 us -> none  [the longest x2 4.06 us: day_cross(): own_re, own_im = (own[..., :bins], own[..., bins:])]
  transfers between devices with their start and end apart: 3 -> 0, of which waited for: 2 -> 0; matrix products, arithmetic and copies ran while one was open for 7% -> 0% of each run, Pallas kernels for 0% -> 0%
where the time goes in v1:
time: 166 us; the launch traced here: 165 us
  Pallas kernels  123 us (74%)
  local copies, waits for them, and re-layouts  30.7 us (18%)
  matrix products  6.45 us (4%)
  other arithmetic  4.96 us (3%)
    pallas_call x1, Pallas kernels, local(): pl.pallas_call(functools.partial(kernel, line, chunks, chans, groups), ou...  123 us
    reshape x4, local copies, waits for them, and re-layouts, packed(): return both.transpose(4, 1, 3, 0, 2).reshape(groups * chans, 4 * windows)  21.3 us
    reshape x1, local copies, waits for them, and re-layouts, local(): summed = summed.reshape(groups, 2, chans // 2, STEPS, 2, chans)  7.1 us
    dot_general x1, matrix products, local(): jnp.einsum('gcishj,chgl->sijl', summed, table, preferred_element_type=jnp...  6.45 us

profile of v1, /device:TPU:0, one launch (start us, length us, event | category | flops | bytes accessed | tf_op | source)
XLA Modules:
  0.0 165.1 jit_solution(1348921830389522122)
XLA Ops:
  0.0 1.5 convert_element_type.15
  1.5 0.5 fusion.8
  2.0 0.5 multiply_convert_fusion
  2.6 0.6 fusion.9
  3.2 0.3 stack.19
  3.4 0.1 copy.28
  3.6 0.3 stack.17
  3.9 0.1 copy.25
  4.0 0.3 stack.16
  4.3 0.1 copy.24
  4.4 1.8 %maximum_bitcast_fusion.1 = (bf16[100,32,2,2,32]{0,4,2,1,3:T(8,128)(2,1)}, bf16[100,32,2,2,32]{0,4,2,1,3:T(8,128)(2,1)}) fusion(bf16[1,32,32,2,100]{4,2,3,1,0:T(8,128)(2,1)S(1)} %copy.28, bf16[1,32,32,2,100]{4,2,3,1,0:T(8,128)(2,1)S(1)} %copy.25, bf16[1,32,32,2,100]{4,2,3,1,0:T(8,128)(2,1)S(1)} %copy.24), kind=kLoop, calls=%fused_computation.6 | loop fusion | flops 819200 | bytes 2867200 | tf_op jit(solution)/shard_map/transpose | solution.py:292
  6.2 8.2 %copy.37 = bf16[100,32,2,2,32]{4,3,2,1,0:T(2,128)(2,1)S(1)} copy(bf16[100,32,2,2,32]{0,4,2,1,3:T(8,128)(2,1)} %get-tuple-element.7) | data formatting | bytes 1638400 | tf_op jit(solution)/shard_map/reshape | solution.py:292
  14.5 2.4 %reshape.33.b_ref = bf16[3200,128]{1,0:T(8,128)(2,1)} reshape(bf16[100,32,2,2,32]{4,3,2,1,0:T(2,128)(2,1)S(1)} %copy.37) | data formatting | bytes 1638400 | tf_op jit(solution)/shard_map/reshape | solution.py:292
  16.9 8.2 %copy.36 = bf16[100,32,2,2,32]{4,3,2,1,0:T(2,128)(2,1)S(1)} copy(bf16[100,32,2,2,32]{0,4,2,1,3:T(8,128)(2,1)} %get-tuple-element.8) | data formatting | bytes 1638400 | tf_op jit(solution)/shard_map/reshape | solution.py:292
  25.1 2.4 %reshape.32.a_ref = bf16[3200,128]{1,0:T(8,128)(2,1)} reshape(bf16[100,32,2,2,32]{4,3,2,1,0:T(2,128)(2,1)S(1)} %copy.36) | data formatting | bytes 1638400 | tf_op jit(solution)/shard_map/reshape | solution.py:292
  27.6 122.8 %shard_map.37 = bf16[3200,128]{1,0:T(8,128)(2,1)} custom-call(s32[2]{0:T(128)} %owners_ref.1, bf16[3200,128]{1,0:T(8,128)(2,1)} %reshape.32.a_ref, bf16[3200,128]{1,0:T(8,128)(2,1)} %reshape.33.b_ref), custom_call_target="tpu_custom_call" | custom-call | tf_op jit(solution)/shard_map/pallas_call | solution.py:301
  150.4 7.1 %reshape.28 = bf16[100,2,16,2,2,32]{5,4,3,2,1,0:T(2,128)(2,1)S(1)} reshape(bf16[3200,128]{1,0:T(8,128)(2,1)} %shard_map.37) | data formatting | bytes 1638400 | tf_op jit(solution)/shard_map/reshape | solution.py:325
  157.5 6.5 %fusion.5 = bf16[2,16,32,400]{3,2,0,1:T(8,128)(2,1)S(1)} fusion(bf16[2,2,100,400,1,1]{2,3,1,0,5,4:T(8,128)(2,1)} %constant.15, bf16[100,2,16,2,2,32]{5,4,3,2,1,0:T(2,128)(2,1)S(1)} %reshape.28), kind=kOutput, calls=%fused_computation.4 | convolution fusion | flops 328499200 | bytes 1958400 | tf_op jit(solution)/shard_map/gcishj,chgl->sijl/dot_general | solution.py:326
  164.0 1.1 copy.33
  (1 shorter events, 0.0 us)

commit v2 on v1

--- a/solution.py
+++ b/solution.py
@@ -11,6 +11,7 @@
 
 LAGS = 400
 STEPS = 2
+LAG = 4
 MESH_ID = pl.DeviceIdType.MESH
 
 
@@ -44,8 +45,8 @@
 
 def kernel(
     line, chunks, chans, groups,
-    owners_ref, a_ref, b_ref, o_ref,
-    w_ref, r1_ref, s2_ref, r2_ref, zout_ref, zin_ref, c_send, c_recv,
+    owners_ref, a_ref, o_ref,
+    b_ref, w_ref, r1_ref, s2_ref, r2_ref, zout_ref, zin_ref, c_send, c_recv,
     send_sem, recv_sem, day_send, day_recv,
 ):
     me = lax.axis_index("chan")
@@ -140,6 +141,27 @@
         for k, step in pairs:
             scatter_first(step, part, k).start()
 
+    lanes_all = a_ref.shape[1]
+    quarter = lanes_all // 4
+    from_lane = lax.broadcasted_iota(jnp.int32, (lanes_all, lanes_all), 0)
+    to_lane = lax.broadcasted_iota(jnp.int32, (lanes_all, lanes_all), 1)
+    is_re = lax.rem(to_lane // quarter, 2) == 0
+    turn = jnp.where(
+        is_re,
+        jnp.where(from_lane == to_lane + quarter, 1.0, 0.0),
+        jnp.where(from_lane + quarter == to_lane, -1.0, 0.0),
+    ).astype(jnp.bfloat16)
+    block_rows = rows // 5 if rows % 80 == 0 else rows
+
+    def turn_rows(i, carry):
+        some = pl.ds(pl.multiple_of(i * block_rows, 16), block_rows)
+        b_ref[some] = jnp.dot(
+            a_ref[some], turn, preferred_element_type=jnp.float32
+        ).astype(jnp.bfloat16)
+        return carry
+
+    lax.fori_loop(0, rows // block_rows, turn_rows, 0)
+
     for k, step in pairs:
         ca, cb, _, _ = coords[step]
         scatter_first(step, 0, k).wait_recv()
@@ -150,10 +172,10 @@
         )
         scatter_second(step, k).start()
 
-    for k, step in pairs:
+    def ready(k, step):
         ca, cb, _, _ = coords[step]
         here = pl.ds(k * size, size)
-        first, second, level, below = hits[step]
+        first, second, _, _ = hits[step]
         scatter_first(step, 1, k).wait_recv()
         scatter_second(step, k).wait_recv()
         mine = jnp.where(
@@ -166,44 +188,52 @@
         own = at((ca * 2 + cb) * piece, k)
         w_ref[step, own] = mine
 
-        def upward():
-            @pl.when(has_left)
-            def _():
-                along(step, k, True).wait_recv()
-                got = zin_ref[0, step, here]
-                zout_ref[0, step, here] = jnp.where(level, zout_ref[0, step, here], got)
-                w_ref[step, own] = jnp.where(below, got, w_ref[step, own])
-
-            @pl.when(has_right)
-            def _():
-                along(step, k, True).start()
-
-        def downward():
-            @pl.when(has_right)
-            def _():
-                along(step, k, False).wait_recv()
-                got = zin_ref[1, step, here]
-                zout_ref[1, step, here] = jnp.where(level, zout_ref[1, step, here], got)
-                w_ref[step, own] = jnp.where(
-                    level, w_ref[step, own], jnp.where(below, w_ref[step, own], got)
-                )
-
-            @pl.when(has_left)
-            def _():
-                along(step, k, False).start()
-
+    def stream(k, step, up):
+        ca, cb, _, _ = coords[step]
+        here = pl.ds(k * size, size)
+        own = at((ca * 2 + cb) * piece, k)
+        _, _, level, below = hits[step]
+        side = 0 if up else 1
+        source = below if up else jnp.logical_not(jnp.logical_or(level, below))
+
+        @pl.when(has_left if up else has_right)
+        def _():
+            along(step, k, up).wait_recv()
+            got = zin_ref[side, step, here]
+            zout_ref[side, step, here] = jnp.where(level, zout_ref[side, step, here], got)
+            w_ref[step, own] = jnp.where(source, got, w_ref[step, own])
+
+        @pl.when(has_right if up else has_left)
+        def _():
+            along(step, k, up).start()
+
+    def both_ways(near, far):
         @pl.when(cz < line // 2)
         def _():
-            upward()
-            downward()
+            if near is not None:
+                stream(*near, True)
+            if far is not None:
+                stream(*far, False)
 
         @pl.when(cz >= line // 2)
         def _():
-            downward()
-            upward()
-
-        gather(step, k, 5).start()
-        gather(step, k, 6).start()
+            if near is not None:
+                stream(*near, False)
+            if far is not None:
+                stream(*far, True)
+
+    count = len(pairs)
+    for tick in range(count + LAG):
+        near = far = None
+        if tick < count:
+            near = pairs[tick]
+            ready(*near)
+        if tick >= LAG:
+            far = pairs[tick - LAG]
+        both_ways(near, far)
+        if far is not None:
+            gather(far[1], far[0], 5).start()
+            gather(far[1], far[0], 6).start()
 
     for k, step in pairs:
         gather(step, k, 5).wait_recv()
@@ -287,12 +317,12 @@
     windows_all = windows * lax.axis_size("day")
     re_part, im_part = whiten(spectra, bins)
 
-    def packed(first, second):
-        both = jnp.stack([first, second], axis=0).reshape(2, chans, windows, 2, groups)
-        return both.transpose(4, 1, 3, 0, 2).reshape(groups * chans, 4 * windows)
-
-    plain = packed(re_part, im_part)
-    turned = packed(im_part, -re_part)
+    plain = jnp.concatenate(
+        [re_part[..., :groups], im_part[..., :groups], re_part[..., groups:], im_part[..., groups:]],
+        axis=1,
+    )
+    plain = lax.optimization_barrier(plain)
+    plain = plain.transpose(2, 0, 1).reshape(groups * chans, 4 * windows)
     rows, lanes = plain.shape
     piece = rows // 4
     chunks = chunks_of(piece)
@@ -301,9 +331,10 @@
     summed = pl.pallas_call(
         functools.partial(kernel, line, chunks, chans, groups),
         out_shape=jax.ShapeDtypeStruct((groups * chans, 4 * chans), bf16),
-        in_specs=[pl.BlockSpec(memory_space=pltpu.SMEM), vmem, vmem],
+        in_specs=[pl.BlockSpec(memory_space=pltpu.SMEM), vmem],
         out_specs=vmem,
         scratch_shapes=[
+            pltpu.VMEM((rows, lanes), bf16),
             pltpu.VMEM((STEPS, rows, lanes), bf16),
             pltpu.VMEM((STEPS, 2, piece, lanes), bf16),
             pltpu.VMEM((STEPS, piece, lanes), bf16),
@@ -318,14 +349,19 @@
             pltpu.SemaphoreType.DMA((4,)),
         ],
         compiler_params=pltpu.CompilerParams(collective_id=0, has_side_effects=True),
-    )(owners, plain, turned)
+    )(owners, plain)
 
     norm = 1.0 / math.sqrt(windows_all * bins)
-    table = jnp.asarray(lag_table(bins, LAGS)).reshape(2, 2, groups, LAGS)
-    summed = summed.reshape(groups, 2, chans // 2, STEPS, 2, chans)
-    lagged = jnp.einsum(
-        "gcishj,chgl->sijl", summed, table, preferred_element_type=jnp.float32
-    ) * norm
+    table = jnp.asarray(lag_table(bins, LAGS))
+    half = chans // 2
+    turned = summed.reshape(groups, chans, 4 * chans).transpose(1, 2, 0)
+    turned = lax.optimization_barrier(turned).reshape(2, half, STEPS, 2, chans, groups)
+    full = jnp.concatenate(
+        [turned[part, :, :, which] for part in range(2) for which in range(2)], axis=-1
+    )
+    full = full.transpose(1, 0, 2, 3).reshape(STEPS * half * chans, 2 * bins)
+    lagged = jnp.dot(full, table, preferred_element_type=jnp.float32) * norm
+    lagged = lagged.reshape(STEPS, half, chans, LAGS)
     return lagged.astype(bf16)
 
 

time: 166 us -> 84.6 us (0.51)
  Pallas kernels: 123 us -> 74.6 us
  local copies, waits for them, and re-layouts: 30.7 us -> 5.58 us
  matrix products: 6.45 us -> 0.64 us
    pallas_call x1, Pallas kernels: 123 us -> 74.6 us  [local(): pl.pallas_call(functools.partial(kernel, line, chunks, chans, groups), ou...]
    reshape x5 -> x1, local copies, waits for them, and re-layouts: 28.4 us -> 1.87 us  [local(): turned = summed.reshape(groups, chans, 4 * chans).transpose(1, 2, 0)]
    dot_general x1, matrix products: 6.45 us -> 0.64 us  [local(): lagged = jnp.dot(full, table, preferred_element_type=jnp.float32) * norm]
where the time goes in v2:
time: 84.6 us; the launch traced here: 84.4 us
  Pallas kernels  74.6 us (88%)
  local copies, waits for them, and re-layouts  5.58 us (7%)
  other arithmetic  3.47 us (4%)
    pallas_call x1, Pallas kernels, local(): pl.pallas_call(functools.partial(kernel, line, chunks, chans, groups), ou...  74.6 us
    reshape x1, local copies, waits for them, and re-layouts, local(): turned = summed.reshape(groups, chans, 4 * chans).transpose(1, 2, 0)  1.87 us

profile of v2, /device:TPU:0, one launch (start us, length us, event | category | flops | bytes accessed | tf_op | source)
XLA Modules:
  0.0 84.4 jit_solution(13998052318671739488)
XLA Ops:
  0.0 1.5 %convert_element_type.15 = f32[32,32,400]{2,1,0:T(8,128)S(1)} convert(bf16[32,32,400]{2,1,0:T(8,128)(2,1)} %param.3) | non-fusion elementwise | flops 409600 | bytes 2457600 | tf_op jit(solution)/shard_map/convert_element_type | solution.py:19
  1.5 0.5 fusion
  2.0 0.6 multiply_convert_fusion.2
  2.6 0.3 fusion.1
  2.9 0.3 pad_maximum_fusion
  3.2 1.6 %copy.9 = bf16[100,32,128]{2,1,0:T(8,128)(2,1)} copy(bf16[100,32,128]{0,2,1:T(8,128)(2,1)S(1)} %bitcast.24) | data formatting | bytes 1638400 | tf_op jit(solution)/shard_map/transpose | solution.py:325
  4.8 74.6 %shard_map.37 = bf16[3200,128]{1,0:T(8,128)(2,1)} custom-call(s32[2]{0:T(128)} %owners_ref.1, bf16[3200,128]{1,0:T(8,128)(2,1)} %bitcast.25), custom_call_target="tpu_custom_call" | custom-call | tf_op jit(solution)/shard_map/pallas_call | solution.py:331
  79.4 1.9 %copy.10 = bf16[100,32,128]{0,2,1:T(8,128)(2,1)S(1)} copy(bf16[100,32,128]{2,1,0:T(8,128)(2,1)} %bitcast.26) | data formatting | bytes 1638400 | tf_op jit(solution)/shard_map/reshape | solution.py:357
  81.3 0.1 slice_bitcast_fusion.3
  81.5 0.0 copy-start
  81.5 0.6 maximum_bitcast_fusion
  82.1 0.1 copy.13
  82.1 0.3 copy-done
  82.5 0.6 multiply_convert_fusion
  83.1 1.3 %copy.14 = bf16[1024,400]{1,0:T(8,128)(2,1)} copy(bf16[1024,400]{0,1:T(8,128)(2,1)S(1)} %multiply_convert_fusion) | data formatting | bytes 1638400 | tf_op jit(solution)/shard_map/convert_element_type | solution.py:365
  (1 shorter events, 0.0 us)
Async XLA Ops:
  81.5 1.0 %copy-start = (bf16[400,400]{1,0:T(8,128)(2,1)S(1)}, bf16[400,400]{1,0:T(8,128)(2,1)}, u32[]{:S(2)}) copy-start(bf16[400,400]{1,0:T(8,128)(2,1)} %constant.13.clone) | copy-start | bytes 960004

commit v3 on v2

--- a/solution.py
+++ b/solution.py
@@ -11,7 +11,7 @@
 
 LAGS = 400
 STEPS = 2
-LAG = 4
+LAG = 10
 MESH_ID = pl.DeviceIdType.MESH
 
 

time: 84.6 us -> 60 us (0.71)
  Pallas kernels: 74.6 us -> 50 us
    pallas_call x1, Pallas kernels: 74.6 us -> 50 us  [local(): pl.pallas_call(functools.partial(kernel, line, chunks, chans, groups), ou...]
where the time goes in v3:
time: 60 us; the launch traced here: 59.8 us
  Pallas kernels  50 us (83%)
  local copies, waits for them, and re-layouts  5.58 us (9%)
  other arithmetic  3.47 us (6%)
  matrix products  0.64 us (1%)
    pallas_call x1, Pallas kernels, local(): pl.pallas_call(functools.partial(kernel, line, chunks, chans, groups), ou...  50 us
    reshape x1, local copies, waits for them, and re-layouts, local(): turned = summed.reshape(groups, chans, 4 * chans).transpose(1, 2, 0)  1.87 us
    transpose x1, local copies, waits for them, and re-layouts, local(): plain = plain.transpose(2, 0, 1).reshape(groups * chans, 4 * windows)  1.58 us
    convert_element_type x1, other arithmetic, whiten(): values = spectra.astype(jnp.float32)  1.5 us
    convert_element_type x1, local copies, waits for them, and re-layouts, local(): return lagged.astype(bf16)  1.3 us

profile of v3, /device:TPU:0, one launch (start us, length us, event | category | flops | bytes accessed | tf_op | source)
XLA Modules:
  0.0 59.8 jit_solution(10323683454198178752)
XLA Ops:
  0.0 1.5 %convert_element_type.15 = f32[32,32,400]{2,1,0:T(8,128)S(1)} convert(bf16[32,32,400]{2,1,0:T(8,128)(2,1)} %param.3) | non-fusion elementwise | flops 409600 | bytes 2457600 | tf_op jit(solution)/shard_map/convert_element_type | solution.py:19
  1.5 0.5 fusion
  2.0 0.6 multiply_convert_fusion.2
  2.6 0.3 fusion.1
  2.9 0.3 pad_maximum_fusion
  3.2 1.6 %copy.9 = bf16[100,32,128]{2,1,0:T(8,128)(2,1)} copy(bf16[100,32,128]{0,2,1:T(8,128)(2,1)S(1)} %bitcast.24) | data formatting | bytes 1638400 | tf_op jit(solution)/shard_map/transpose | solution.py:325
  4.8 50.0 %shard_map.37 = bf16[3200,128]{1,0:T(8,128)(2,1)} custom-call(s32[2]{0:T(128)} %owners_ref.1, bf16[3200,128]{1,0:T(8,128)(2,1)} %bitcast.25), custom_call_target="tpu_custom_call" | custom-call | tf_op jit(solution)/shard_map/pallas_call | solution.py:331
  54.8 1.9 %copy.10 = bf16[100,32,128]{0,2,1:T(8,128)(2,1)S(1)} copy(bf16[100,32,128]{2,1,0:T(8,128)(2,1)} %bitcast.26) | data formatting | bytes 1638400 | tf_op jit(solution)/shard_map/reshape | solution.py:357
  56.7 0.1 slice_bitcast_fusion.3
  56.8 0.0 copy-start
  56.8 0.6 maximum_bitcast_fusion
  57.4 0.1 copy.13
  57.5 0.3 copy-done
  57.8 0.6 %multiply_convert_fusion = bf16[1024,400]{0,1:T(8,128)(2,1)S(1)} fusion(bf16[1024,400]{1,0:T(8,128)(2,1)S(1)} %bitcast.27, bf16[400,400]{1,0:T(8,128)(2,1)S(1)} %copy-done), kind=kOutput, calls=%fused_computation | convolution fusion | flops 328499200 | bytes 1958400 | tf_op jit(solution)/shard_map/dot_general | solution.py:363
  58.5 1.3 %copy.14 = bf16[1024,400]{1,0:T(8,128)(2,1)} copy(bf16[1024,400]{0,1:T(8,128)(2,1)S(1)} %multiply_convert_fusion) | data formatting | bytes 1638400 | tf_op jit(solution)/shard_map/convert_element_type | solution.py:365
  (1 shorter events, 0.0 us)
Async XLA Ops:
  56.8 1.0 %copy-start = (bf16[400,400]{1,0:T(8,128)(2,1)S(1)}, bf16[400,400]{1,0:T(8,128)(2,1)}, u32[]{:S(2)}) copy-start(bf16[400,400]{1,0:T(8,128)(2,1)} %constant.13.clone) | copy-start | bytes 960004

commit v4 on v3

--- a/solution.py
+++ b/solution.py
@@ -360,6 +360,7 @@
         [turned[part, :, :, which] for part in range(2) for which in range(2)], axis=-1
     )
     full = full.transpose(1, 0, 2, 3).reshape(STEPS * half * chans, 2 * bins)
+    full = lax.optimization_barrier(full)
     lagged = jnp.dot(full, table, preferred_element_type=jnp.float32) * norm
     lagged = lagged.reshape(STEPS, half, chans, LAGS)
     return lagged.astype(bf16)

time: 60 us -> 60 us (level)
  no operation moved by 1% of the time
where the time goes in v4:
time: 60 us; the launch traced here: 59.8 us
  Pallas kernels  50 us (83%)
  local copies, waits for them, and re-layouts  5.58 us (9%)
  other arithmetic  3.47 us (6%)
  matrix products  0.64 us (1%)
    pallas_call x1, Pallas kernels, local(): pl.pallas_call(functools.partial(kernel, line, chunks, chans, groups), ou...  50 us
    reshape x1, local copies, waits for them, and re-layouts, local(): turned = summed.reshape(groups, chans, 4 * chans).transpose(1, 2, 0)  1.87 us
    transpose x1, local copies, waits for them, and re-layouts, local(): plain = plain.transpose(2, 0, 1).reshape(groups * chans, 4 * windows)  1.58 us
    convert_element_type x1, other arithmetic, whiten(): values = spectra.astype(jnp.float32)  1.5 us
    convert_element_type x1, local copies, waits for them, and re-layouts, local(): return lagged.astype(bf16)  1.3 us

profile of v4, /device:TPU:0, one launch (start us, length us, event | category | flops | bytes accessed | tf_op | source)
XLA Modules:
  0.0 59.8 jit_solution(10323683454198178752)
XLA Ops:
  0.0 1.5 %convert_element_type.15 = f32[32,32,400]{2,1,0:T(8,128)S(1)} convert(bf16[32,32,400]{2,1,0:T(8,128)(2,1)} %param.3) | non-fusion elementwise | flops 409600 | bytes 2457600 | tf_op jit(solution)/shard_map/convert_element_type | solution.py:19
  1.5 0.5 fusion
  2.0 0.6 multiply_convert_fusion.2
  2.6 0.3 fusion.1
  2.9 0.3 pad_maximum_fusion
  3.2 1.6 %copy.9 = bf16[100,32,128]{2,1,0:T(8,128)(2,1)} copy(bf16[100,32,128]{0,2,1:T(8,128)(2,1)S(1)} %bitcast.24) | data formatting | bytes 1638400 | tf_op jit(solution)/shard_map/transpose | solution.py:325
  4.8 50.0 %shard_map.37 = bf16[3200,128]{1,0:T(8,128)(2,1)} custom-call(s32[2]{0:T(128)} %owners_ref.1, bf16[3200,128]{1,0:T(8,128)(2,1)} %bitcast.25), custom_call_target="tpu_custom_call" | custom-call | tf_op jit(solution)/shard_map/pallas_call | solution.py:331
  54.8 1.9 %copy.10 = bf16[100,32,128]{0,2,1:T(8,128)(2,1)S(1)} copy(bf16[100,32,128]{2,1,0:T(8,128)(2,1)} %bitcast.26) | data formatting | bytes 1638400 | tf_op jit(solution)/shard_map/reshape | solution.py:357
  56.7 0.1 slice_bitcast_fusion.3
  56.8 0.0 copy-start
  56.8 0.6 maximum_bitcast_fusion
  57.4 0.1 copy.13
  57.5 0.3 copy-done
  57.8 0.6 %multiply_convert_fusion = bf16[1024,400]{0,1:T(8,128)(2,1)S(1)} fusion(bf16[1024,400]{1,0:T(8,128)(2,1)S(1)} %bitcast.27, bf16[400,400]{1,0:T(8,128)(2,1)S(1)} %copy-done), kind=kOutput, calls=%fused_computation | convolution fusion | flops 328499200 | bytes 1958400 | tf_op jit(solution)/shard_map/dot_general | solution.py:364
  58.5 1.3 %copy.14 = bf16[1024,400]{1,0:T(8,128)(2,1)} copy(bf16[1024,400]{0,1:T(8,128)(2,1)S(1)} %multiply_convert_fusion) | data formatting | bytes 1638400 | tf_op jit(solution)/shard_map/convert_element_type | solution.py:366
  (1 shorter events, 0.0 us)
Async XLA Ops:
  56.8 1.0 %copy-start = (bf16[400,400]{1,0:T(8,128)(2,1)S(1)}, bf16[400,400]{1,0:T(8,128)(2,1)}, u32[]{:S(2)}) copy-start(bf16[400,400]{1,0:T(8,128)(2,1)} %constant.13.clone) | copy-start | bytes 960004
